TPU v7x, 32 devices: a whole 2x2x4 slice. The times are simulated.
32 devices in a mesh: seq: 8 (over z, core), grp: 2 (over y), dp: 2 (over x).
Axes of the slice: x: 2, y: 2, z: 4, core: 2. Of those that a mesh axis runs over, the one named last changes fastest.
Arguments:
- clips: bfloat16 [2, 1024, 1408], P('dp', 'seq'), may hold values from -6 to 6
- context: int32 [2, 1024], P('dp', 'seq'), may hold values from 0 to 1, as said below
- predict_index: int32 [2, 1536], P('dp', 'seq'), may hold values from -1 to 1023, as said below
- target_qkv: bfloat16 [3, 1408, 1408], P(None, 'dp', 'grp'), may hold values from -8 to 8
- target_out: bfloat16 [1408, 1408], P('grp'), may hold values from -0.15625 to 0.15625
- student_qkv: bfloat16 [3, 1408, 1408], P(None, 'dp', 'grp'), may hold values from -8 to 8
- student_out: bfloat16 [1408, 1408], P('grp', 'dp'), may hold values from -0.15625 to 0.15625
- mask_token: float32 [1408], replicated, may hold values from -4 to 4
Outputs:
- out_grad: float32 [1408, 1408], P('grp', 'dp')
- target_blend: float32 [1408, 1408], P('grp')
Inputs may be any that keep to these rules, and one draw needn't show every extreme that they name: In every aligned block of 128 tokens of a clip exactly 32 tokens have context 1 and the others 0. `predict_index`: each device's 192 slots name distinct target positions (context 0) of its clip, followed by -1 in the unused slots; different devices' lists may name the same position. In every clip one list is full.
All inputs are finite; a program needn't handle non-finite values.
Results may differ from a plain program's by a relative error of at most 0.014.
Values may be sent and summed in bfloat16 or wider, within the bound.
A program may use at most 128 MiB of HBM per device.

v0:
```python
import math
import jax
import jax.numpy as jnp
from jax import lax
from jax.sharding import PartitionSpec as P

HEAD_DIM = 88
CTX_DEV = 32
EPSILON = 1e-06
MOMENTUM = 0.99


def layer_norm(values):
    center = values - jnp.mean(values, axis=-1, keepdims=True)
    factor = lax.rsqrt(jnp.mean(center * center, axis=-1, keepdims=True) + EPSILON)
    return (center * factor, factor)


def position_table(places, width):
    half_width = width // 2
    spacing = jnp.exp(jnp.arange(half_width, dtype=jnp.float32) * (-math.log(10000.0) / half_width))
    angles = places.astype(jnp.float32)[:, None] * spacing[None, :]
    return jnp.concatenate([jnp.sin(angles), jnp.cos(angles)], axis=1)


def to_heads(queries):
    head_count = queries.shape[1] // HEAD_DIM
    return queries.reshape(queries.shape[0], head_count, HEAD_DIM).transpose(1, 0, 2)


def empty_state(head_count, row_count):
    peaks = jnp.full((head_count, row_count), -1e30, jnp.float32)
    totals = jnp.zeros((head_count, row_count), jnp.float32)
    summed = jnp.zeros((head_count, row_count, HEAD_DIM), jnp.float32)
    return (peaks, totals, summed)


def from_heads(running):
    peaks, totals, summed = running
    mixed = summed / totals[:, :, None]
    head_count, row_count, unused = mixed.shape
    return mixed.transpose(1, 0, 2).reshape(row_count, head_count * HEAD_DIM).astype(jnp.bfloat16)


def attend_shard(running, shard_rows, query_heads):
    peaks, totals, summed = running
    key_rows, value_rows = shard_rows
    length = key_rows.shape[0]
    head_count = query_heads.shape[0]
    key_heads = key_rows.reshape(length, head_count, HEAD_DIM)
    value_heads = value_rows.reshape(length, head_count, HEAD_DIM)
    factor = HEAD_DIM ** (-0.5)
    scores = (
        jnp.einsum("hqd,khd->hqk", query_heads, key_heads, preferred_element_type=jnp.float32)
        * factor
    )
    raised = jnp.maximum(peaks, jnp.max(scores, axis=2))
    shifted = jnp.exp(scores - raised[:, :, None])
    totals = jnp.sum(shifted, axis=2)
    summed = jnp.einsum(
        "hqk,khd->hqd",
        shifted.astype(jnp.bfloat16),
        value_heads,
        preferred_element_type=jnp.float32,
    )
    return (raised, totals, summed)


def body(
    clips, context, predict_index, target_qkv, target_out, student_qkv, student_out, mask_token
):
    tokens = clips[0]
    keep_flags = context[0]
    listed = predict_index[0]
    row_count, width = tokens.shape
    half_width = target_qkv.shape[2]
    head_count = half_width // HEAD_DIM
    normed = layer_norm(tokens.astype(jnp.float32))[0].astype(jnp.bfloat16)
    projected = jnp.einsum(
        "nr,krc->knc",
        normed,
        lax.all_gather(target_qkv, "dp", axis=1, tiled=True),
        preferred_element_type=jnp.float32,
    )
    projected = projected.astype(jnp.bfloat16)
    target_state = attend_shard(
        empty_state(head_count, row_count),
        (
            lax.all_gather(projected[1], "seq", axis=0, tiled=True),
            lax.all_gather(projected[2], "seq", axis=0, tiled=True),
        ),
        query_heads=to_heads(projected[0]),
    )
    target_mixed = from_heads(target_state)
    target_part = jnp.dot(target_mixed, target_out, preferred_element_type=jnp.float32)
    target_sum = lax.psum(target_part.astype(jnp.bfloat16), "grp").astype(jnp.float32)
    features = layer_norm(tokens.astype(jnp.float32) + target_sum)[0].astype(jnp.bfloat16)
    first_row = lax.axis_index("seq") * row_count
    every_list = lax.all_gather(listed, "seq", axis=0, tiled=True)
    places = first_row + jnp.arange(row_count, dtype=jnp.int32)
    usable = jnp.sum((every_list[None, :] == places[:, None]).astype(jnp.float32), axis=1)
    slot_count = places.shape[0]
    is_context = keep_flags == 1
    context_order = jnp.cumsum(is_context.astype(jnp.int32)) - 1
    selector = (
        (context_order[None, :] == jnp.arange(CTX_DEV, dtype=jnp.int32)[:, None])
        & is_context[None, :]
    ).astype(jnp.bfloat16)
    context_rows = jnp.dot(selector, normed, preferred_element_type=jnp.float32).astype(
        jnp.bfloat16
    )
    seeds = mask_token[None, :] + position_table(jnp.maximum(places, 0), width)
    seed_normed = layer_norm(seeds)[0].astype(jnp.bfloat16)
    shard_rows = lax.all_gather(student_qkv, "dp", axis=1, tiled=True)
    query_total = jnp.dot(seed_normed, shard_rows[0], preferred_element_type=jnp.float32)
    pair_total = jnp.einsum(
        "nr,krc->knc", context_rows, shard_rows[1:], preferred_element_type=jnp.float32
    )
    student_pairs = pair_total
    student_pairs = student_pairs.astype(jnp.bfloat16)
    student_state = attend_shard(
        empty_state(head_count, slot_count),
        (
            lax.all_gather(student_pairs[0], "seq", axis=0, tiled=True),
            lax.all_gather(student_pairs[1], "seq", axis=0, tiled=True),
        ),
        query_heads=to_heads(query_total.astype(jnp.bfloat16)),
    )
    student_mixed = from_heads(student_state)
    relaid = lax.all_gather(student_out, "dp", axis=1, tiled=True)
    student_part = jnp.dot(student_mixed, relaid, preferred_element_type=jnp.float32)
    student_sum = lax.psum(student_part.astype(jnp.bfloat16), "grp").astype(jnp.float32)
    predicted, factor = layer_norm(seeds + student_sum)
    wanted = features.astype(jnp.float32)
    slope = jnp.clip(predicted - wanted, -1.0, 1.0) * usable[:, None]
    back_grad = (
        slope
        - jnp.mean(slope, axis=1, keepdims=True)
        - predicted * jnp.mean(slope * predicted, axis=1, keepdims=True)
    ) * factor
    local_grad = jnp.dot(
        student_mixed.astype(jnp.float32).T, back_grad, precision=lax.Precision.HIGHEST
    )
    column_grad = lax.psum_scatter(
        local_grad.astype(jnp.bfloat16), "dp", scatter_dimension=1, tiled=True
    )
    out_grad = lax.psum(column_grad, "seq").astype(jnp.float32)
    target_blend = MOMENTUM * target_out.astype(jnp.float32) + (1.0 - MOMENTUM) * relaid.astype(
        jnp.float32
    )
    return (out_grad, target_blend)


def solution(mesh):
    in_specs = (
        P("dp", "seq", None),
        P("dp", "seq"),
        P("dp", "seq"),
        P(None, "dp", "grp"),
        P("grp", None),
        P(None, "dp", "grp"),
        P("grp", "dp"),
        P(),
    )
    out_specs = (P("grp", "dp"), P("grp", None))
    return jax.shard_map(body, mesh=mesh, in_specs=in_specs, out_specs=out_specs, check_vma=False)
```

profile of v0, /device:TPU:0, one launch (start us, length us, event | category | flops | bytes accessed | tf_op | source)
XLA Modules:
  0.0 480.1 jit_solution(4295476264770077709)
XLA Ops:
  7.2 6.9 %copy.48 = bf16[3,704,704]{2,0,1:T(4,128)(2,1)} copy(bf16[3,704,704]{2,1,0:T(8,128)(2,1)} %param.11) | data formatting | bytes 5947392 | tf_op args[3]
  14.2 4.8 %copy.41 = bf16[3,704,704]{2,0,1:T(4,128)(2,1)} copy(bf16[3,704,704]{2,1,0:T(8,128)(2,1)S(1)} %copy-done.5) | data formatting | bytes 5947392 | tf_op args[5]
  20.3 1.5 copy.47
  22.2 104.2 %all-gather.15.cloned.1.call-done = bf16[3,1408,704]{2,0,1:T(4,128)(2,1)} async-done(((bf16[3,704,704]{2,0,1:T(4,128)(2,1)}), bf16[3,1408,704]{2,0,1:T(4,128)(2,1)}) %all-gather.15.cloned.1.call-update) | async-done | bytes 5947408 | tf_op jit(solution)/shard_map/all_gather | solution.py:82
  126.4 6.0 %fusion.16 = bf16[3,128,704]{1,2,0:T(8,128)(2,1)S(1)} fusion(bf16[3,1408,704]{2,0,1:T(4,128)(2,1)} %all-gather.15.cloned.1.call-done, bf16[1,128,1408]{2,1,0:T(8,128)(2,1)S(1)} %copy-done.1, f32[128]{0:T(128)S(1)} %add_rsqrt_fusion.2, f32[128]{0:T(128)S(1)} %broadcast_multiply_fusion.4), kind=kOutput, calls=%fused_computation.21 | convolution fusion | flops 762257408 | bytes 6849536 | tf_op jit(solution)/shard_map/nr,krc->knc/dot_general | solution.py:79
  133.9 1.4 multiply_sine_fusion
  135.9 101.4 %all-gather.11.cloned.1.call-done = bf16[3,1408,704]{2,0,1:T(4,128)(2,1)} async-done(((bf16[3,704,704]{2,0,1:T(4,128)(2,1)}), bf16[3,1408,704]{2,0,1:T(4,128)(2,1)}) %all-gather.11.cloned.1.call-update) | async-done | bytes 5947408 | tf_op jit(solution)/shard_map/all_gather | solution.py:114
  237.3 7.6 %slice.29 = bf16[2,1408,704]{2,0,1:T(2,128)(2,1)} slice(bf16[3,1408,704]{2,0,1:T(4,128)(2,1)} %all-gather.11.cloned.1.call-done), slice={[1:3], [0:1408], [0:704]} | slice | bytes 7929856 | tf_op jit(solution)/shard_map/slice | solution.py:117
  244.9 3.7 fusion.30
  249.3 14.5 %all-gather.1 = bf16[1,256,704]{2,1,0:T(8,128)(2,1)S(1)} all-gather(bf16[1,32,704]{2,1,0:T(8,128)(2,1)S(1)} %get-tuple-element.19), channel_id=3, replica_groups=mesh['seq'=8,'grp'=2,'dp'=2] {'seq'}, dimensions={1}, use_global_device_ids=true | all-gather | bytes 405504 | tf_op jit(solution)/shard_map/all_gather | solution.py:125
  264.7 7.1 %slice.28 = bf16[1,1408,704]{2,0,1:T(2,128)(2,1)} slice(bf16[3,1408,704]{2,0,1:T(4,128)(2,1)} %all-gather.11.cloned.1.call-done), slice={[0:1], [0:1408], [0:704]} | slice | bytes 3964928 | tf_op jit(solution)/shard_map/slice | solution.py:115
  271.7 12.0 %copy.54 = bf16[1,1408,704]{1,2,0:T(8,128)(2,1)S(1)} copy(bf16[1,1408,704]{2,0,1:T(2,128)(2,1)} %slice.28) | data formatting | bytes 3964928
  283.8 16.5 %all-gather = bf16[1,256,704]{2,1,0:T(8,128)(2,1)S(1)} all-gather(bf16[1,32,704]{2,1,0:T(8,128)(2,1)} %get-tuple-element.18), channel_id=2, replica_groups=mesh['seq'=8,'grp'=2,'dp'=2] {'seq'}, dimensions={1}, use_global_device_ids=true | all-gather | bytes 405504 | tf_op jit(solution)/shard_map/all_gather | solution.py:124
  302.0 1.4 fusion.85
  304.3 3.2 convolution_convert_fusion.2
  307.5 2.2 multiply_reduce_fusion
  309.7 1.9 copy-done
  312.5 18.5 %all-gather.19.cloned.1.call-done = bf16[1,1024,704]{1,2,0:T(8,128)(2,1)} async-done(((bf16[1,128,704]{1,2,0:T(8,128)(2,1)}), bf16[1,1024,704]{1,2,0:T(8,128)(2,1)}) %all-gather.19.cloned.1.call-update) | async-done | bytes 1441808 | tf_op jit(solution)/shard_map/all_gather | solution.py:90
  331.0 3.6 fusion.36
  334.7 1.2 convolution_convert_fusion.1
  337.6 7.6 %all-reduce = s32[1536]{0:T(1024)S(1)} all-reduce(s32[1536]{0:T(1024)S(1)} %dynamic-update-slice), channel_id=6, replica_groups=mesh['seq'=8,'grp'=2,'dp'=2] {'seq'}, use_global_device_ids=true, to_apply=%add | all-reduce | flops 1536 | bytes 12288
  345.4 22.1 %all-reduce.7.cloned.1.call-done = (bf16[128,1408]{1,0:T(8,128)(2,1)}, bf16[128,1408]{1,0:T(8,128)(2,1)}) async-done(((bf16[128,1408]{1,0:T(8,128)(2,1)}, bf16[128,1408]{1,0:T(8,128)(2,1)}), (bf16[128,1408]{1,0:T(8,128)(2,1)}, bf16[128,1408]{1,0:T(8,128)(2,1)})) %all-reduce.7.cloned.1.call-update) | async-done | bytes 720912 | tf_op jit(solution)/shard_map/psum | solution.py:96
  368.8 1.4 fusion.82
  371.0 2.0 convolution_convert_fusion
  373.0 2.5 copy.52
  375.6 4.1 copy.50
  379.7 28.6 %reduce-scatter.4.cloned.1.call-done = bf16[704,704]{1,0:T(8,128)(2,1)} async-done(((bf16[1408,704]{1,0:T(8,128)(2,1)}), bf16[704,704]{1,0:T(8,128)(2,1)}) %reduce-scatter.4.cloned.1.call-update) | async-done | bytes 991248
  408.3 2.3 copy.53
  410.7 4.3 multiply_add_fusion
  415.0 5.6 %copy.51 = f32[704,1408]{1,0:T(8,128)} copy(f32[704,1408]{0,1:T(8,128)} %multiply_add_fusion) | data formatting | bytes 7929856
  420.6 49.9 %all-reduce.5.cloned.1.call-done = bf16[704,704]{1,0:T(8,128)(2,1)} async-done(((bf16[704,704]{1,0:T(8,128)(2,1)}), bf16[704,704]{1,0:T(8,128)(2,1)}) %all-reduce.5.cloned.1.call-update) | async-done | bytes 991248 | tf_op jit(solution)/shard_map/psum | solution.py:147
  470.5 2.7 convert_element_type.121
  (81 shorter events, 12.0 us)
Async XLA Ops:
  7.2 7.1 %copy-start.5 = (bf16[3,704,704]{2,1,0:T(8,128)(2,1)S(1)}, bf16[3,704,704]{2,1,0:T(8,128)(2,1)}, u32[]{:S(2)}) copy-start(bf16[3,704,704]{2,1,0:T(8,128)(2,1)} %param.13) | copy-start | bytes 8921092
  7.2 119.2 %all-gather.15.cloned.1.call-start = ((), (), s32[]{:S(2)}) async-start(), calls=%async_computation.3 | async-start | bytes 12976128 | tf_op jit(solution)/shard_map/all_gather | solution.py:82
  14.2 223.2 %all-gather.11.cloned.1.call-start = ((), (), s32[]{:S(2)}) async-start(), calls=%async_computation.1 | async-start | bytes 12976128 | tf_op jit(solution)/shard_map/all_gather | solution.py:114
  19.0 1.2 copy-start.6
  19.0 2.8 copy-start.1
  19.1 285.2 %all-gather.13.cloned.1.call-start = ((), (), s32[]{:S(2)}) async-start(), calls=%async_computation.2 | async-start | bytes 3244032 | tf_op jit(solution)/shard_map/all_gather | solution.py:130
  21.8 285.7 %all-gather.17.cloned.1.call-start = ((), (), s32[]{:S(2)}) async-start(), calls=%async_computation.5 | async-start | bytes 1622016 | tf_op jit(solution)/shard_map/all_gather | solution.py:89
  22.2 111.3 %copy-start.11 = (s32[1,128]{1,0:T(1,128)S(1)}, s32[1,128]{1,0:T(1,128)}, u32[]{:S(2)}) copy-start(s32[1,128]{1,0:T(1,128)} %param.9) | copy-start | bytes 1540
  22.2 113.1 %copy-start.9 = (f32[1408]{0:T(1024)S(1)}, f32[1408]{0:T(1024)}, u32[]{:S(2)}) copy-start(f32[1408]{0:T(1024)} %param.15) | copy-start | bytes 16900
  133.2 197.8 %all-gather.19.cloned.1.call-start = ((), (), s32[]{:S(2)}) async-start(), calls=%async_computation.6 | async-start | bytes 1622016 | tf_op jit(solution)/shard_map/all_gather | solution.py:90
  283.8 83.8 %all-reduce.7.cloned.1.call-start = ((), (), s32[]{:S(2)}) async-start(), calls=%async_computation.8 | async-start | bytes 1441792 | tf_op jit(solution)/shard_map/psum | solution.py:96
  301.2 2.6 copy-start.8
  302.0 5.5 %copy-start.7 = (bf16[1,128,704]{1,2,0:T(8,128)(2,1)S(1)}, bf16[1,128,704]{1,2,0:T(8,128)(2,1)}, u32[]{:S(2)}) copy-start(bf16[1,128,704]{1,2,0:T(8,128)(2,1)} %get-tuple-element.17) | copy-start | bytes 540676
  309.7 1.9 copy-start
  312.5 22.2 %copy-start.3 = (bf16[704,1408]{1,0:T(8,128)(2,1)S(1)}, bf16[704,1408]{1,0:T(8,128)(2,1)}, u32[]{:S(2)}) copy-start(bf16[704,1408]{1,0:T(8,128)(2,1)} %param.12) | copy-start | bytes 5947396
  331.0 5.0 %copy-start.12 = (u32[32]{0:T(128)S(1)}, u32[32]{0:T(128)}, u32[]{:S(2)}) copy-start(u32[32]{0:T(128)} %constant.55) | copy-start | bytes 388
  331.0 6.3 %copy-start.10 = (s32[1,192]{1,0:T(1,128)S(1)}, s32[1,192]{1,0:T(1,128)}, u32[]{:S(2)}) copy-start(s32[1,192]{1,0:T(1,128)} %param.10) | copy-start | bytes 2308
  336.0 72.4 %reduce-scatter.4.cloned.1.call-start = ((), (), s32[]{:S(2)}) async-start(), calls=%async_computation.7 | async-start | bytes 3244032
  367.6 2.9 copy-start.4
  375.5 35.1 %copy-start.2 = (bf16[704,1408]{0,1:T(8,128)(2,1)S(1)}, bf16[704,1408]{0,1:T(8,128)(2,1)}, u32[]{:S(2)}) copy-start(bf16[704,1408]{0,1:T(8,128)(2,1)} %all-gather.13.cloned.1.call-done) | copy-start | bytes 5947396
  375.5 95.0 %all-reduce.5.cloned.1.call-start = ((), (), s32[]{:S(2)}) async-start(), calls=%async_computation.4 | async-start | bytes 2162688 | tf_op jit(solution)/shard_map/psum | solution.py:147
Sparse Core Ops, SparseCore 0:
  14.3 112.0 all-gather.14
  128.0 109.3 all-gather.10
  239.5 33.8 all-gather.12
  274.8 28.2 all-gather.16
  304.5 26.4 all-gather.18
  336.1 31.4 all-reduce.6
  375.7 32.6 reduce-scatter.3
  411.2 59.2 all-reduce.4
where the time goes:
time: 481 us; the launch traced here: 480 us
  waiting for transfers between devices  325 us (68%)
  local copies, waits for them, and re-layouts  61.8 us (13%)
  blocking collectives  38.6 us (8%)
  matrix products  24.5 us (5%)
  between operations  15.1 us (3%)
  other arithmetic  14.7 us (3%)
    all_gather x1, waiting for transfers between devices, body(): lax.all_gather(target_qkv, 'dp', axis=1, tiled=True)  104 us
    all_gather x1, waiting for transfers between devices, body(): shard_rows = lax.all_gather(student_qkv, 'dp', axis=1, tiled=True)  101 us
    psum x1, waiting for transfers between devices, body(): out_grad = lax.psum(column_grad, 'seq').astype(jnp.float32)  49.9 us
    unnamed x37, local copies, waits for them, and re-layouts  43.8 us
    unnamed x9, waiting for transfers between devices  28.7 us
    psum x1, waiting for transfers between devices, body(): lax.psum(target_part.astype(jnp.bfloat16), 'grp').astype(jnp.float32)  22.1 us
    all_gather x1, waiting for transfers between devices, body(): lax.all_gather(projected[2], 'seq', axis=0, tiled=True)  18.5 us
    all_gather x1, blocking collectives, body(): lax.all_gather(student_pairs[0], 'seq', axis=0, tiled=True)  16.5 us
  transfers between devices with their start and end apart: 8, of which 6 were waited for; matrix products, arithmetic and copies ran while one was open for 15% of the time, Pallas kernels for 0%

commit v1 on v0

--- a/solution.py
+++ b/solution.py
@@ -144,7 +144,7 @@
     column_grad = lax.psum_scatter(
         local_grad.astype(jnp.bfloat16), "dp", scatter_dimension=1, tiled=True
     )
-    out_grad = lax.psum(column_grad, "seq").astype(jnp.float32)
+    out_grad = jnp.sum(lax.all_gather(column_grad, "seq"), axis=0).astype(jnp.float32)
     target_blend = MOMENTUM * target_out.astype(jnp.float32) + (1.0 - MOMENTUM) * relaid.astype(
         jnp.float32
     )

time: 481 us -> 510 us (1.060)
  waiting for transfers between devices: 325 us -> 349 us
    all_gather x0 -> x1, waiting for transfers between devices: none -> 70.4 us  [body(): lax.all_gather(column_grad, 'seq')]
    psum x1 -> x0, waiting for transfers between devices: 49.9 us -> none  [body(): out_grad = lax.psum(column_grad, 'seq').astype(jnp.float32)]
    reduce_sum x0 -> x1, other arithmetic: none -> 5.41 us  [body(): jnp.sum(lax.all_gather(column_grad, 'seq'), axis=0).astype(jnp.float32)]
    unnamed x37 -> x35, local copies, waits for them, and re-layouts: 43.8 us -> 44.4 us
where the time goes in v1:
time: 510 us; the launch traced here: 509 us
  waiting for transfers between devices  349 us (68%)
  local copies, waits for them, and re-layouts  62.4 us (12%)
  blocking collectives  38.6 us (8%)
  matrix products  24.5 us (5%)
  other arithmetic  18.9 us (4%)
  between operations  15 us (3%)
    all_gather x1, waiting for transfers between devices, body(): lax.all_gather(target_qkv, 'dp', axis=1, tiled=True)  103 us
    all_gather x1, waiting for transfers between devices, body(): shard_rows = lax.all_gather(student_qkv, 'dp', axis=1, tiled=True)  101 us
    all_gather x1, waiting for transfers between devices, body(): lax.all_gather(column_grad, 'seq')  70.4 us
    unnamed x35, local copies, waits for them, and re-layouts  44.4 us
    unnamed x9, waiting for transfers between devices  32.8 us
    psum x1, waiting for transfers between devices, body(): lax.psum(target_part.astype(jnp.bfloat16), 'grp').astype(jnp.float32)  22.2 us
    all_gather x1, waiting for transfers between devices, body(): lax.all_gather(projected[2], 'seq', axis=0, tiled=True)  18.7 us
    all_gather x1, blocking collectives, body(): lax.all_gather(student_pairs[0], 'seq', axis=0, tiled=True)  16.5 us
  transfers between devices with their start and end apart: 8, of which 6 were waited for; matrix products, arithmetic and copies ran while one was open for 15% of the time, Pallas kernels for 0%

profile of v1, /device:TPU:0, one launch (start us, length us, event | category | flops | bytes accessed | tf_op | source)
XLA Modules:
  0.0 508.8 jit_solution(9201925751202005182)
XLA Ops:
  7.2 6.8 %copy.48 = bf16[3,704,704]{2,0,1:T(4,128)(2,1)} copy(bf16[3,704,704]{2,1,0:T(8,128)(2,1)} %param.11) | data formatting | bytes 5947392 | tf_op args[3]
  14.1 6.8 %copy.41 = bf16[3,704,704]{2,0,1:T(4,128)(2,1)} copy(bf16[3,704,704]{2,1,0:T(8,128)(2,1)} %param.13) | data formatting | bytes 5947392 | tf_op args[5]
  20.9 1.5 copy.47
  22.9 103.3 %all-gather.17.cloned.1.call-done = bf16[3,1408,704]{2,0,1:T(4,128)(2,1)} async-done(((bf16[3,704,704]{2,0,1:T(4,128)(2,1)}), bf16[3,1408,704]{2,0,1:T(4,128)(2,1)}) %all-gather.17.cloned.1.call-update) | async-done | bytes 5947408 | tf_op jit(solution)/shard_map/all_gather | solution.py:82
  126.2 6.0 %fusion.16 = bf16[3,128,704]{1,2,0:T(8,128)(2,1)S(1)} fusion(bf16[3,1408,704]{2,0,1:T(4,128)(2,1)} %all-gather.17.cloned.1.call-done, bf16[1,128,1408]{2,1,0:T(8,128)(2,1)S(1)} %copy-done.1, f32[128]{0:T(128)S(1)} %add_rsqrt_fusion.2, f32[128]{0:T(128)S(1)} %broadcast_multiply_fusion.4), kind=kOutput, calls=%fused_computation.21 | convolution fusion | flops 762257408 | bytes 6849536 | tf_op jit(solution)/shard_map/nr,krc->knc/dot_general | solution.py:79
  133.7 1.4 multiply_sine_fusion
  135.7 101.5 %all-gather.13.cloned.1.call-done = bf16[3,1408,704]{2,0,1:T(4,128)(2,1)} async-done(((bf16[3,704,704]{2,0,1:T(4,128)(2,1)}), bf16[3,1408,704]{2,0,1:T(4,128)(2,1)}) %all-gather.13.cloned.1.call-update) | async-done | bytes 5947408 | tf_op jit(solution)/shard_map/all_gather | solution.py:114
  237.2 7.6 %slice.29 = bf16[2,1408,704]{2,0,1:T(2,128)(2,1)} slice(bf16[3,1408,704]{2,0,1:T(4,128)(2,1)} %all-gather.13.cloned.1.call-done), slice={[1:3], [0:1408], [0:704]} | slice | bytes 7929856 | tf_op jit(solution)/shard_map/slice | solution.py:117
  244.7 3.7 fusion.30
  249.1 14.5 %all-gather.1 = bf16[1,256,704]{2,1,0:T(8,128)(2,1)S(1)} all-gather(bf16[1,32,704]{2,1,0:T(8,128)(2,1)S(1)} %get-tuple-element.19), channel_id=3, replica_groups=mesh['seq'=8,'grp'=2,'dp'=2] {'seq'}, dimensions={1}, use_global_device_ids=true | all-gather | bytes 405504 | tf_op jit(solution)/shard_map/all_gather | solution.py:125
  264.5 7.1 %slice.28 = bf16[1,1408,704]{2,0,1:T(2,128)(2,1)} slice(bf16[3,1408,704]{2,0,1:T(4,128)(2,1)} %all-gather.13.cloned.1.call-done), slice={[0:1], [0:1408], [0:704]} | slice | bytes 3964928 | tf_op jit(solution)/shard_map/slice | solution.py:115
  271.5 12.0 %copy.54 = bf16[1,1408,704]{1,2,0:T(8,128)(2,1)S(1)} copy(bf16[1,1408,704]{2,0,1:T(2,128)(2,1)} %slice.28) | data formatting | bytes 3964928
  283.6 16.5 %all-gather = bf16[1,256,704]{2,1,0:T(8,128)(2,1)S(1)} all-gather(bf16[1,32,704]{2,1,0:T(8,128)(2,1)} %get-tuple-element.18), channel_id=2, replica_groups=mesh['seq'=8,'grp'=2,'dp'=2] {'seq'}, dimensions={1}, use_global_device_ids=true | all-gather | bytes 405504 | tf_op jit(solution)/shard_map/all_gather | solution.py:124
  301.8 1.4 fusion.85
  304.1 3.2 convolution_convert_fusion.2
  307.3 2.2 multiply_reduce_fusion
  309.5 1.9 copy-done
  312.4 18.7 %all-gather.21.cloned.1.call-done = bf16[1,1024,704]{1,2,0:T(8,128)(2,1)} async-done(((bf16[1,128,704]{1,2,0:T(8,128)(2,1)}), bf16[1,1024,704]{1,2,0:T(8,128)(2,1)}) %all-gather.21.cloned.1.call-update) | async-done | bytes 1441808 | tf_op jit(solution)/shard_map/all_gather | solution.py:90
  331.1 3.6 fusion.36
  337.6 7.6 %all-reduce = s32[1536]{0:T(1024)S(1)} all-reduce(s32[1536]{0:T(1024)S(1)} %dynamic-update-slice), channel_id=6, replica_groups=mesh['seq'=8,'grp'=2,'dp'=2] {'seq'}, use_global_device_ids=true, to_apply=%add | all-reduce | flops 1536 | bytes 12288
  345.5 22.2 %all-reduce.4.cloned.1.call-done = (bf16[128,1408]{1,0:T(8,128)(2,1)}, bf16[128,1408]{1,0:T(8,128)(2,1)}) async-done(((bf16[128,1408]{1,0:T(8,128)(2,1)}, bf16[128,1408]{1,0:T(8,128)(2,1)}), (bf16[128,1408]{1,0:T(8,128)(2,1)}, bf16[128,1408]{1,0:T(8,128)(2,1)})) %all-reduce.4.cloned.1.call-update) | async-done | bytes 720912 | tf_op jit(solution)/shard_map/psum | solution.py:96
  368.9 1.4 fusion.82
  371.1 2.0 convolution_convert_fusion
  373.1 2.5 copy.52
  375.6 32.7 %reduce-scatter.4.cloned.1.call-done = bf16[704,704]{1,0:T(8,128)(2,1)} async-done(((bf16[1408,704]{1,0:T(8,128)(2,1)}), bf16[704,704]{1,0:T(8,128)(2,1)}) %reduce-scatter.4.cloned.1.call-update) | async-done | bytes 991248
  408.4 2.3 copy.53
  410.7 4.0 copy.50
  414.7 4.4 multiply_add_fusion
  419.1 5.7 %copy.51 = f32[704,1408]{1,0:T(8,128)} copy(f32[704,1408]{0,1:T(8,128)} %multiply_add_fusion) | data formatting | bytes 7929856
  424.7 70.4 %all-gather.23.cloned.1.call-done = bf16[5632,704]{1,0:T(8,128)(2,1)} async-done(((bf16[704,704]{1,0:T(8,128)(2,1)}), bf16[5632,704]{1,0:T(8,128)(2,1)}) %all-gather.23.cloned.1.call-update) | async-done | bytes 7929872 | tf_op jit(solution)/shard_map/all_gather | solution.py:147
  495.1 5.4 %reduce_sum.142 = bf16[704,704]{1,0:T(8,128)(2,1)S(1)} reduce(bf16[8,704,704]{2,1,0:T(8,128)(2,1)} %bitcast.90, bf16[]{:T(256)} %constant.49.clone.1), dimensions={0}, to_apply=%region_19.20 | reduce | flops 3469312 | bytes 8921090 | tf_op jit(solution)/shard_map/reduce_sum | solution.py:147
  500.5 1.5 convert_element_type.123
  (80 shorter events, 12.1 us)
Async XLA Ops:
  7.2 119.1 %all-gather.17.cloned.1.call-start = ((), (), s32[]{:S(2)}) async-start(), calls=%async_computation.3 | async-start | bytes 12976128 | tf_op jit(solution)/shard_map/all_gather | solution.py:82
  14.0 6.9 %copy-start.5 = (bf16[704,704]{1,0:T(8,128)(2,1)S(1)}, bf16[704,704]{1,0:T(8,128)(2,1)}, u32[]{:S(2)}) copy-start(bf16[704,704]{1,0:T(8,128)(2,1)} %param.14) | copy-start | bytes 2973700
  14.0 223.2 %all-gather.13.cloned.1.call-start = ((), (), s32[]{:S(2)}) async-start(), calls=%async_computation.1 | async-start | bytes 12976128 | tf_op jit(solution)/shard_map/all_gather | solution.py:114
  20.9 1.6 copy-start.1
  20.9 283.2 %all-gather.15.cloned.1.call-start = ((), (), s32[]{:S(2)}) async-start(), calls=%async_computation.2 | async-start | bytes 3244032 | tf_op jit(solution)/shard_map/all_gather | solution.py:130
  22.5 284.8 %all-gather.19.cloned.1.call-start = ((), (), s32[]{:S(2)}) async-start(), calls=%async_computation.4 | async-start | bytes 1622016 | tf_op jit(solution)/shard_map/all_gather | solution.py:89
  22.9 110.4 %copy-start.10 = (s32[1,128]{1,0:T(1,128)S(1)}, s32[1,128]{1,0:T(1,128)}, u32[]{:S(2)}) copy-start(s32[1,128]{1,0:T(1,128)} %param.9) | copy-start | bytes 1540
  22.9 112.2 %copy-start.8 = (f32[1408]{0:T(1024)S(1)}, f32[1408]{0:T(1024)}, u32[]{:S(2)}) copy-start(f32[1408]{0:T(1024)} %param.15) | copy-start | bytes 16900
  133.0 198.0 %all-gather.21.cloned.1.call-start = ((), (), s32[]{:S(2)}) async-start(), calls=%async_computation.5 | async-start | bytes 1622016 | tf_op jit(solution)/shard_map/all_gather | solution.py:90
  283.6 84.0 %all-reduce.4.cloned.1.call-start = ((), (), s32[]{:S(2)}) async-start(), calls=%async_computation.8 | async-start | bytes 1441792 | tf_op jit(solution)/shard_map/psum | solution.py:96
  301.1 2.6 copy-start.7
  301.8 5.5 %copy-start.6 = (bf16[1,128,704]{1,2,0:T(8,128)(2,1)S(1)}, bf16[1,128,704]{1,2,0:T(8,128)(2,1)}, u32[]{:S(2)}) copy-start(bf16[1,128,704]{1,2,0:T(8,128)(2,1)} %get-tuple-element.17) | copy-start | bytes 540676
  309.5 1.9 copy-start
  312.3 22.4 %copy-start.3 = (bf16[704,1408]{1,0:T(8,128)(2,1)S(1)}, bf16[704,1408]{1,0:T(8,128)(2,1)}, u32[]{:S(2)}) copy-start(bf16[704,1408]{1,0:T(8,128)(2,1)} %param.12) | copy-start | bytes 5947396
  331.1 5.0 copy-start.11
  331.1 6.3 %copy-start.9 = (s32[1,192]{1,0:T(1,128)S(1)}, s32[1,192]{1,0:T(1,128)}, u32[]{:S(2)}) copy-start(s32[1,192]{1,0:T(1,128)} %param.10) | copy-start | bytes 2308
  336.0 72.4 %reduce-scatter.4.cloned.1.call-start = ((), (), s32[]{:S(2)}) async-start(), calls=%async_computation.7 | async-start | bytes 3244032
  367.6 2.9 copy-start.4
  375.6 39.1 %copy-start.2 = (bf16[704,1408]{0,1:T(8,128)(2,1)S(1)}, bf16[704,1408]{0,1:T(8,128)(2,1)}, u32[]{:S(2)}) copy-start(bf16[704,1408]{0,1:T(8,128)(2,1)} %all-gather.15.cloned.1.call-done) | copy-start | bytes 5947396
  375.6 119.5 %all-gather.23.cloned.1.call-start = ((), (), s32[]{:S(2)}) async-start(), calls=%async_computation.6 | async-start | bytes 9732096 | tf_op jit(solution)/shard_map/all_gather | solution.py:147
Sparse Core Ops, SparseCore 0:
  14.1 112.0 all-gather.16
  127.8 109.3 all-gather.12
  239.3 33.8 all-gather.14
  274.6 28.2 all-gather.18
  304.3 26.6 all-gather.20
  336.1 31.4 all-reduce.3
  375.7 32.6 reduce-scatter.3
  410.8 84.2 all-gather.22
